TPU v7x, 1024 devices: a whole 8x8x8 slice. The times are simulated.
1024 devices in a mesh: clip: 32 (over y_hi, x), seq: 16 (over y_lo, z), tp: 2 (over core).
Axes of the slice: x: 8, y: 8 (y_hi: 4, y_lo: 2; y = y_hi * 2 + y_lo), z: 8, core: 2. Of those that a mesh axis runs over, the one named last changes fastest.
Arguments:
- ffn_hidden: bfloat16 [4096, 10240], P('clip', 'tp'), may hold values from -6 to 6
- ffn_weight: bfloat16 [10240, 4096], P('tp', 'seq'), may hold values from -0.0625 to 0.0625
- residual: bfloat16 [4096, 4096], P('clip', 'seq'), may hold values from -6 to 6
- norm_gain: float32 [4096], replicated, may hold values from 0.3 to 3
- kv_weight: bfloat16 [4096, 32, 256], P(None, ('seq', 'tp')), may hold values from -0.09375 to 0.09375
- destination: int32 [4096, 1], replicated, may hold values from 0 to 31; in each aligned block of 128 rows (0 to 127, 128 to 255, ...) at most 16 rows name the same one
- queries: bfloat16 [131072, 4096], P(('clip', 'seq', 'tp')), may hold values from -360 to 360
Outputs:
- attended: bfloat16 [131072, 4096], P(('clip', 'seq', 'tp'))
Inputs may be any that keep to these rules, and one draw needn't show every extreme that they name: `destination`: in each aligned block of 128 rows no clip is named by more than 16 rows, a bound that some block reaches; every clip is named by some row.
All inputs are finite; a program needn't handle non-finite values.
Results may differ from a plain program's by a relative error of at most 0.01375.
The roundings to bfloat16 on the way count: a program that leaves them out, or rounds other values in their place, can miss the bound.
Values may be sent and summed in bfloat16 or wider, within the bound.
A program may use at most 64 MiB of HBM per device.

v0:
```python
import math

import jax
import jax.numpy as jnp
from jax import lax
from jax.sharding import PartitionSpec as P

EPSILON = 1e-06


def slot_table(dest_block, clips, capacity):
    onehot = (dest_block[:, None] == jnp.arange(clips, dtype=jnp.int32)[None, :]).astype(jnp.int32)
    before = jnp.cumsum(onehot, axis=0) - onehot
    rank = jnp.sum(before * onehot, axis=1)
    target = jnp.arange(clips * capacity, dtype=jnp.int32)
    select = (dest_block[None, :] == (target // capacity)[:, None]) & (
        rank[None, :] == (target % capacity)[:, None]
    )
    return select.astype(jnp.bfloat16)


def live_slots(dest_all, clip_now, clips, capacity, rows):
    counts = jnp.sum((dest_all.reshape(clips, rows) == clip_now).astype(jnp.int32), axis=1)
    return (jnp.arange(capacity, dtype=jnp.int32)[None, :] < counts[:, None]).reshape(
        clips * capacity
    )


def normalize(text, gain):
    wide = text.astype(jnp.float32)
    scale = lax.rsqrt(jnp.mean(wide * wide, axis=1, keepdims=True) + EPSILON)
    return (wide * scale * gain[None, :]).astype(jnp.bfloat16)


def attend(query, keyval, valid):
    width = query.shape[-1]
    keys = keyval[:, :, :width]
    values = keyval[:, :, width:]
    scores = jnp.einsum(
        "rhd,shd->hrs", query, keys, preferred_element_type=jnp.float32
    ) / math.sqrt(width)
    scores = jnp.where(valid[None, None, :], scores, -1e30)
    peak = jnp.max(scores, axis=2, keepdims=True)
    weights = jnp.where(valid[None, None, :], jnp.exp(scores - peak), 0.0)
    probs = (weights / jnp.sum(weights, axis=2, keepdims=True)).astype(jnp.bfloat16)
    return jnp.einsum("hrs,shd->rhd", probs, values, preferred_element_type=jnp.float32).astype(
        jnp.bfloat16
    )


def shards(ffn_hidden, ffn_weight, residual, norm_gain, kv_weight, destination, queries):
    clips = lax.axis_size("clip")
    rows = ffn_hidden.shape[0]
    capacity = rows // min(8, clips)
    heads_here = kv_weight.shape[1]
    head_dim = kv_weight.shape[2] // 2
    weight_flat = kv_weight.reshape(kv_weight.shape[0], heads_here * 2 * head_dim)
    partial_value = jnp.dot(ffn_hidden, ffn_weight, preferred_element_type=jnp.float32)
    summed = lax.psum(partial_value, "tp")
    text = (residual.astype(jnp.float32) + summed).astype(jnp.bfloat16)
    here = lax.axis_index("clip")
    dest_all = destination[:, 0]
    dest_block = lax.dynamic_slice_in_dim(dest_all, here * rows, rows)
    select = slot_table(dest_block, clips, capacity)
    valid = live_slots(dest_all, here, clips, capacity, rows)
    packed = jnp.dot(select, text, preferred_element_type=jnp.float32).astype(jnp.bfloat16)
    packed = packed.reshape(clips, capacity, text.shape[1])
    arrived = lax.all_to_all(packed, "clip", split_axis=0, concat_axis=0, tiled=True)
    arrived = arrived.reshape(clips * capacity, text.shape[1])
    full_text = lax.all_gather(arrived, "seq", axis=1, tiled=True)
    normed = normalize(full_text, norm_gain)
    keyval = jnp.dot(normed, weight_flat, preferred_element_type=jnp.float32).astype(jnp.bfloat16)
    keyval = keyval.reshape(clips * capacity, heads_here, 2 * head_dim)
    token_rows, width_all = queries.shape
    block = min(16, token_rows)
    stacked = queries.reshape(token_rows // block, block, width_all)
    gathered = lax.all_to_all(stacked, ("seq", "tp"), split_axis=2, concat_axis=1, tiled=True)
    count = gathered.shape[0]
    flat = gathered.reshape(-1, heads_here, head_dim)
    result = attend(flat, keyval, valid).reshape(count, -1, heads_here * head_dim)
    output = lax.all_to_all(result, ("seq", "tp"), split_axis=1, concat_axis=2, tiled=True)
    return output.reshape(token_rows, width_all)


def solution(mesh):
    return jax.shard_map(
        shards,
        mesh=mesh,
        in_specs=(
            P("clip", "tp"),
            P("tp", "seq"),
            P("clip", "seq"),
            P(),
            P(None, ("seq", "tp"), None),
            P(),
            P(("clip", "seq", "tp"), None),
        ),
        out_specs=P(("clip", "seq", "tp"), None),
        check_vma=False,
    )
```

profile of v0, /device:TPU:1, one launch (start us, length us, event | category | flops | bytes accessed | tf_op | source)
XLA Modules:
  0.0 262.5 jit_solution(17990734963082459749)
XLA Ops:
  6.5 1.7 copy-done
  8.3 2.5 fusion.39
  10.8 0.7 dynamic-slice_bitcast_fusion
  11.6 0.2 reduce_window_sum.11
  12.0 54.2 %all-reduce.2.cloned.1.call-done = f32[128,256]{1,0:T(8,128)} async-done(((f32[128,256]{1,0:T(8,128)}), f32[128,256]{1,0:T(8,128)}) %all-reduce.2.cloned.1.call-update) | async-done | bytes 131088 | tf_op jit(solution)/shard_map/psum | solution.py:59
  66.2 1.2 convolution_convert_fusion.1
  67.4 21.7 %all_to_all.35 = bf16[32,16,256]{2,1,0:T(8,128)(2,1)} all-to-all(bf16[32,16,256]{2,1,0:T(8,128)(2,1)S(1)} %bitcast.56), channel_id=1, replica_groups=mesh['clip'=32,'seq'=16,'tp'=2] {'clip'}, dimensions={0} | all-to-all | bytes 524288 | tf_op jit(solution)/shard_map/all_to_all | solution.py:68
  89.2 8.2 %copy.19 = bf16[8,16,4096]{1,0,2:T(8,128)(2,1)} copy(bf16[8,16,4096]{2,1,0:T(8,128)(2,1)} %bitcast.55) | data formatting | bytes 2097152 | tf_op jit(solution)/shard_map/reshape | solution.py:76
  97.4 11.2 %reshape.124 = bf16[32,2,8192]{2,1,0:T(2,128)(2,1)} reshape(bf16[4096,8,16]{2,1,0:T(8,128)(2,1)} %bitcast.50) | data formatting | bytes 2097152
  108.6 11.6 %all-to-all-start.1 = ((bf16[32,2,8192]{2,1,0:T(2,128)(2,1)}), bf16[32,2,8192]{2,1,0:T(2,128)(2,1)}, u32[]{:S(2)}, u32[]{:S(2)}) async-start(bf16[32,2,8192]{2,1,0:T(2,128)(2,1)} %reshape.124), calls=%async_computation.1 | async-start | bytes 2097152 | tf_op jit(solution)/shard_map/all_to_all | solution.py:77
  120.5 31.9 %all-to-all-done.1 = bf16[32,2,8192]{2,1,0:T(2,128)(2,1)} async-done(((bf16[32,2,8192]{2,1,0:T(2,128)(2,1)}), bf16[32,2,8192]{2,1,0:T(2,128)(2,1)}, u32[]{:S(2)}, u32[]{:S(2)}) %all-to-all-start.1) | async-done | bytes 1048608 | tf_op jit(solution)/shard_map/all_to_all | solution.py:77
  152.4 8.9 %reshape.125 = bf16[4096,8,16]{2,1,0:T(8,128)(2,1)} reshape(bf16[32,2,8192]{2,1,0:T(2,128)(2,1)} %all-to-all-done.1) | data formatting | bytes 2097152
  161.3 8.7 %copy.21 = bf16[8,32,16,128]{3,2,1,0:T(8,128)(2,1)} copy(bf16[8,32,16,128]{2,0,3,1:T(8,128)(2,1)} %bitcast.49) | data formatting | bytes 2097152 | tf_op jit(solution)/shard_map/all_to_all | solution.py:77
  170.0 20.7 %all-gather.2.cloned.1.call-done = bf16[512,4096]{1,0:T(8,128)(2,1)} async-done(((bf16[512,256]{1,0:T(8,128)(2,1)}), bf16[512,4096]{1,0:T(8,128)(2,1)}) %all-gather.2.cloned.1.call-update) | async-done | bytes 4194320 | tf_op jit(solution)/shard_map/all_gather | solution.py:70
  190.6 3.2 %fusion = f32[512]{0:T(512)S(1)} fusion(bf16[512,4096]{1,0:T(8,128)(2,1)} %all-gather.2.cloned.1.call-done), kind=kLoop, calls=%fused_computation.2 | loop fusion | flops 6290944 | bytes 4196352 | tf_op jit(solution)/shard_map/reduce_sum | solution.py:31
  193.8 4.2 %fusion.15 = bf16[512,1,256]{2,0,1:T(8,128)(2,1)S(1)} fusion(bf16[4096,1,256]{2,0,1:T(8,128)(2,1)} %param.11, bf16[512,4096]{1,0:T(8,128)(2,1)} %all-gather.2.cloned.1.call-done, f32[4096]{0:T(1024)S(1)} %copy-done.3, f32[512]{0:T(512)S(1)} %add_rsqrt_fusion), kind=kOutput, calls=%fused_computation.17 | convolution fusion | flops 1082261504 | bytes 6572032 | tf_op jit(solution)/shard_map/dot_general | solution.py:72
  198.0 1.4 fusion.3
  199.4 2.5 fusion.4
  201.9 2.7 %convolution_convert_fusion = bf16[128,4096]{1,0:T(8,128)(2,1)S(1)} fusion(f32[512,4096]{1,0:T(8,128)S(1)} %get-tuple-element.6, f32[4096]{0:T(1024)S(1)} %fusion.4, f32[4096]{0:T(1024)S(1)} %get-tuple-element.5, pred[512]{0:T(512)(128)(4,1)S(1)} %lt.34, bf16[512,1,256]{2,0,1:T(8,128)(2,1)S(1)} %fusion.15), kind=kOutput, calls=%fused_computation.10 | convolution fusion | flops 549978112 | bytes 9601536 | tf_op jit(solution)/shard_map/hrs,shd->rhd/dot_general | solution.py:46
  204.5 1.4 copy.28
  205.9 3.0 %copy.22 = bf16[8,512,128]{2,0,1:T(8,128)(2,1)} copy(bf16[8,512,128]{1,0,2:T(8,128)(2,1)} %bitcast.52) | data formatting | bytes 2097152 | tf_op jit(solution)/shard_map/reshape | solution.py:80
  208.9 44.7 %all_to_all.36 = bf16[8,512,128]{2,0,1:T(8,128)(2,1)S(1)} all-to-all(bf16[8,512,128]{2,0,1:T(8,128)(2,1)} %copy.22), channel_id=1, replica_groups=mesh['clip'=32,'seq'=16,'tp'=2] {'seq','tp'}, dimensions={1} | all-to-all | bytes 2097152 | tf_op jit(solution)/shard_map/all_to_all | solution.py:81
  253.6 0.7 copy.24
  254.3 1.4 copy.31
  (19 shorter events, 0.7 us)
Async XLA Ops:
  6.5 1.7 copy-start
  6.5 59.6 %all-reduce.2.cloned.1.call-start = ((), (), s32[]{:S(2)}) async-start(), calls=%async_computation.3 | async-start | bytes 262144 | tf_op jit(solution)/shard_map/psum | solution.py:59
  10.8 179.9 %all-gather.2.cloned.1.call-start = ((), (), s32[]{:S(2)}) async-start(), calls=%async_computation.4 | async-start | bytes 4456448 | tf_op jit(solution)/shard_map/all_gather | solution.py:70
  89.2 31.0 %copy-start.2 = (s32[4096,1]{0,1:T(1,128)S(1)}, s32[4096,1]{0,1:T(1,128)}, u32[]{:S(2)}) copy-start(s32[4096,1]{0,1:T(1,128)} %param.12) | copy-start | bytes 49156
  108.6 43.8 %all-to-all-start.1 = ((bf16[32,2,8192]{2,1,0:T(2,128)(2,1)}), bf16[32,2,8192]{2,1,0:T(2,128)(2,1)}, u32[]{:S(2)}, u32[]{:S(2)}) async-start(bf16[32,2,8192]{2,1,0:T(2,128)(2,1)} %reshape.124), calls=%async_computation.1 | async-start | bytes 2097152 | tf_op jit(solution)/shard_map/all_to_all | solution.py:77
  161.3 32.5 %copy-start.3 = (f32[4096]{0:T(1024)S(1)}, f32[4096]{0:T(1024)}, u32[]{:S(2)}) copy-start(f32[4096]{0:T(1024)} %param.10) | copy-start | bytes 49156
  190.6 7.4 %copy-start.1 = (bf16[8,32,16,128]{3,2,1,0:T(8,128)(2,1)S(1)}, bf16[8,32,16,128]{3,2,1,0:T(8,128)(2,1)}, u32[]{:S(2)}) copy-start(bf16[8,32,16,128]{3,2,1,0:T(8,128)(2,1)} %copy.21) | copy-start | bytes 3145732
Sparse Core Ops, SparseCore 0:
  10.9 55.2 all-reduce.1
  89.3 101.3 all-gather.1
where the time goes:
time: 264 us; the launch traced here: 263 us
  waiting for transfers between devices  107 us (41%)
  blocking collectives  66.4 us (25%)
  local copies, waits for them, and re-layouts  45.9 us (17%)
  between operations  13.5 us (5%)
  matrix products  11.9 us (5%)
  starting transfers between devices  11.6 us (4%)
  other arithmetic  6.29 us (2%)
    psum x1, waiting for transfers between devices, shards(): summed = lax.psum(partial_value, 'tp')  54.2 us
    all_to_all x1, blocking collectives, shards(): lax.all_to_all(result, ('seq', 'tp'), split_axis=1, concat_axis=2, tiled=...  44.7 us
    all_to_all x1, waiting for transfers between devices, shards(): lax.all_to_all(stacked, ('seq', 'tp'), split_axis=2, concat_axis=1, tiled...  31.9 us
    unnamed x12, local copies, waits for them, and re-layouts  24.6 us
    all_to_all x1, blocking collectives, shards(): lax.all_to_all(packed, 'clip', split_axis=0, concat_axis=0, tiled=True)  21.7 us
    all_gather x1, waiting for transfers between devices, shards(): full_text = lax.all_gather(arrived, 'seq', axis=1, tiled=True)  20.7 us
    all_to_all x1, starting transfers between devices, shards(): lax.all_to_all(stacked, ('seq', 'tp'), split_axis=2, concat_axis=1, tiled...  11.6 us
    all_to_all x1, local copies, waits for them, and re-layouts, shards(): lax.all_to_all(stacked, ('seq', 'tp'), split_axis=2, concat_axis=1, tiled...  8.67 us
  transfers between devices with their start and end apart: 3, of which 3 were waited for; matrix products, arithmetic and copies ran while one was open for 15% of the time, Pallas kernels for 0%

commit v1 on v0

v1 whole, which is shorter than its diff:
```python
import math

import jax
import jax.numpy as jnp
from jax import lax
from jax.experimental import pallas as pl
from jax.experimental.pallas import tpu as pltpu
from jax.sharding import PartitionSpec as P

EPSILON = 1e-06
MESH = pl.DeviceIdType.MESH
F32 = jnp.float32
BF16 = jnp.bfloat16
CAPACITY = 16
ZS = 8


def remote(src, dst, send_sem, recv_sem, device):
    return pltpu.make_async_remote_copy(
        src_ref=src,
        dst_ref=dst,
        send_sem=send_sem,
        recv_sem=recv_sem,
        device_id=device,
        device_id_type=MESH,
    )


def ring_step(k):
    return 4 + (1 - 2 * (k % 2)) * ((k + 1) // 2)


def kernel(
    hid,
    wt,
    res,
    gain,
    kvw,
    dest,
    qry,
    out,
    hid_v,
    wt_v,
    res_v,
    gain_v,
    w2_v,
    dest_v,
    sel_v,
    bias_v,
    part,
    part_in,
    tbuf,
    nbuf,
    kv_out,
    kv_rows,
    packed,
    kvbuf,
    kt_v,
    qbuf,
    rbuf,
    ld,
    tp_s,
    tp_r,
    w_s,
    w_r,
    ag_s,
    ag_r,
    q_s,
    q_r,
    kx_s,
    kx_r,
    c_s,
    c_r,
    r_s,
    r_r,
):
    clips = lax.axis_size("clip")
    group = lax.axis_size("seq") * 2
    c, s, t = lax.axis_index("clip"), lax.axis_index("seq"), lax.axis_index("tp")
    y, z = s // ZS, s % ZS
    me = s * 2 + t
    other = 1 - t
    partner = (c, s, other)
    rows = hid_v.shape[0]
    half = rows // 2
    feat = part.shape[1]
    blocks = tbuf.shape[0]
    hd = 128

    barrier = pltpu.get_barrier_semaphore()

    @pl.loop(1, group)
    def _(o):
        g = (me + o) % group
        pl.semaphore_signal(barrier, inc=1, device_id=(c, g // 2, g % 2), device_id_type=MESH)

    @pl.loop(1, clips)
    def _(o):
        pl.semaphore_signal(barrier, inc=1, device_id=((c + o) % clips, s, t), device_id_type=MESH)

    def column(j):
        return pl.ds(pl.multiple_of(j * hd, hd), hd)

    def block_rows(j, size):
        return pl.ds(pl.multiple_of(j * size, size), size)

    loads = [
        pltpu.make_async_copy(dest, dest_v, ld.at[0]),
        pltpu.make_async_copy(hid, hid_v, ld.at[1]),
        pltpu.make_async_copy(wt, wt_v, ld.at[2]),
        pltpu.make_async_copy(res, res_v, ld.at[3]),
        pltpu.make_async_copy(gain, gain_v, ld.at[4]),
        pltpu.make_async_copy(kvw, w2_v.at[t], ld.at[5]),
        pltpu.make_async_copy(qry.at[:, column(me)], qbuf.at[block_rows(me, rows)], ld.at[6]),
    ]
    for load in loads:
        load.start()

    loads[0].wait()
    dest_row = dest_v[pl.ds(c, 1), :]
    clip_ids = lax.broadcasted_iota(jnp.int32, (clips, rows), 0)
    onehot = jnp.where(clip_ids == dest_row, 1.0, 0.0)
    earlier = jnp.where(
        lax.broadcasted_iota(jnp.int32, (rows, rows), 0)
        < lax.broadcasted_iota(jnp.int32, (rows, rows), 1),
        1.0,
        0.0,
    ).astype(BF16)
    before = jnp.dot(onehot.astype(BF16), earlier, preferred_element_type=F32)
    rank = jnp.sum(before * onehot, axis=0, keepdims=True)
    place = dest_row * CAPACITY + rank.astype(jnp.int32)
    slots = clips * CAPACITY
    target = lax.broadcasted_iota(jnp.int32, (slots, rows), 0)
    sel_v[...] = jnp.where(target == place, 1.0, 0.0).astype(BF16)
    counts = jnp.sum(jnp.where(dest_v[...] == c, 1.0, 0.0), axis=1, keepdims=True)
    slot = lax.broadcasted_iota(jnp.int32, (clips, slots), 1)
    source = lax.broadcasted_iota(jnp.int32, (clips, slots), 0)
    in_block = jnp.where(slot // CAPACITY == source, counts, 0.0)
    filled = jnp.sum(in_block, axis=0, keepdims=True)
    position = (lax.broadcasted_iota(jnp.int32, (1, slots), 1) % CAPACITY).astype(F32)
    bias_v[...] = jnp.where(position < filled, 0.0, -1e30)

    loads[1].wait()
    loads[2].wait()
    step = 1024
    part[...] = jnp.zeros_like(part)

    @pl.loop(0, hid_v.shape[1] // step)
    def _(k):
        at = pl.ds(pl.multiple_of(k * step, step), step)
        part[...] += jnp.dot(hid_v[:, at], wt_v[at, :], preferred_element_type=F32)

    pl.semaphore_wait(barrier, group - 1 + clips - 1)

    tp_copy = remote(part.at[block_rows(other, half)], part_in, tp_s, tp_r, partner)
    tp_copy.start()
    loads[3].wait()
    loads[4].wait()
    tp_copy.wait_recv()
    mine = part[block_rows(t, half), :] + part_in[...]
    text = res_v[block_rows(t, half), :].astype(F32) + mine
    tbuf[s] = text.astype(BF16)

    def text_copy(block, device):
        return remote(tbuf.at[block], tbuf.at[block], ag_s, ag_r.at[block], device)

    across = (1 - y) * ZS + z

    @pl.loop(0, ZS - 1)
    def _(k):
        text_copy(s, (c, y * ZS + (z + ring_step(k)) % ZS, t)).start()

    text_copy(s, (c, across, t)).start()

    def query_copy(k, dy, flip):
        peer_s = ((y + dy) % 2) * ZS + (z + ring_step(k)) % ZS
        peer_t = (t + 1 + flip) % 2
        peer = peer_s * 2 + peer_t
        return remote(
            qry.at[:, column(peer)],
            qbuf.at[block_rows(me, rows)],
            q_s,
            q_r,
            (c, peer_s, peer_t),
        )

    @pl.loop(0, 2 * ZS - 1)
    def _(i):
        query_copy(i // 2, 0, i % 2).start()

    weights = remote(kvw, w2_v.at[t], w_s, w_r, partner)
    weights.start()

    @pl.loop(0, ZS - 1)
    def _(k):
        block = y * ZS + (z + ring_step(ZS - 2 - k)) % ZS
        text_copy(block, (c, across, t)).wait_recv()
        text_copy(block, (c, across, t)).start()

    @pl.loop(0, 2 * ZS)
    def _(i):
        query_copy(i // 2, 1, i % 2).start()

    @pl.loop(0, ZS)
    def _(k):
        text_copy((1 - y) * ZS + k, (c, across, t)).wait_recv()

    def squares(b, acc):
        wide = tbuf[b].astype(F32)
        return acc + wide * wide

    total = lax.fori_loop(0, blocks, squares, jnp.zeros((half, feat), F32))
    mean = jnp.sum(total, axis=1, keepdims=True) / (blocks * feat)
    scale = lax.rsqrt(mean + EPSILON)

    @pl.loop(0, blocks)
    def _(b):
        g = gain_v[:, pl.ds(pl.multiple_of(b * feat, feat), feat)]
        nbuf[b] = (tbuf[b].astype(F32) * scale * g).astype(BF16)

    def project(head):
        def add(b, acc):
            w = w2_v[head, pl.ds(pl.multiple_of(b * feat, feat), feat), :]
            return acc + jnp.dot(nbuf[b], w, preferred_element_type=F32)

        return lax.fori_loop(0, blocks, add, jnp.zeros((half, 2 * hd), F32)).astype(BF16)

    weights.wait_recv()
    kv_out[...] = project(other)
    swap = remote(kv_out, kv_rows.at[block_rows(t, half)], kx_s, kx_r, partner)
    swap.start()
    loads[5].wait()
    kv_rows[block_rows(t, half), :] = project(t)
    remote(kv_out, kv_rows.at[block_rows(other, half)], kx_s, kx_r, partner).wait_recv()

    packed[...] = jnp.dot(sel_v[...], kv_rows[...], preferred_element_type=F32).astype(BF16)

    @pl.loop(0, clips)
    def _(o):
        d = (c + clips // 2 + o) % clips

        @pl.when(d != c)
        def _():
            remote(
                packed.at[block_rows(d, CAPACITY)],
                kvbuf.at[block_rows(c, CAPACITY)],
                c_s,
                c_r,
                (d, s, t),
            ).start()

    kvbuf[block_rows(c, CAPACITY), :] = packed[block_rows(c, CAPACITY), :]

    routed = (clips - 1) * CAPACITY
    slots_in = remote(packed.at[pl.ds(0, routed)], kvbuf.at[pl.ds(0, routed)], c_s, c_r, partner)
    slots_in.wait_recv()
    kt_v[...] = kvbuf[:, :hd].T

    moved = (group - 1) * rows
    queries_in = remote(qry.at[:, pl.ds(0, (group - 1) * hd)], qbuf.at[pl.ds(0, moved)], q_s, q_r, partner)
    queries_in.wait_recv()
    loads[6].wait()

    factor = 1.0 / math.sqrt(hd)

    def pair_of(p):
        return ((y + 1 - p % 2) % 2) * ZS + (z + ring_step(p // 2)) % ZS

    def result_copy(peer_s, peer_t):
        return remote(
            rbuf.at[block_rows(peer_s * 2 + peer_t, rows)],
            out.at[:, column(me)],
            r_s,
            r_r,
            (c, peer_s, peer_t),
        )

    @pl.loop(0, group // 2)
    def _(p):
        peer_s = pair_of(p)
        q = qbuf[block_rows(peer_s, 2 * rows), :]
        scores = jnp.dot(q, kt_v[...], preferred_element_type=F32) * factor + bias_v[...]
        peak = jnp.max(scores, axis=1, keepdims=True)
        w = jnp.exp(scores - peak)
        probs = (w * (1.0 / jnp.sum(w, axis=1, keepdims=True))).astype(BF16)
        attended = jnp.dot(probs, kvbuf[:, hd:], preferred_element_type=F32)
        rbuf[block_rows(peer_s, 2 * rows), :] = attended.astype(BF16)

        @pl.when(p > 0)
        def _():
            sent = pair_of(p - 1)
            result_copy(sent, other).start()
            result_copy(sent, t).start()

    result_copy(s, other).start()
    own = pltpu.make_async_copy(rbuf.at[block_rows(me, rows)], out.at[:, column(me)], ld.at[7])
    own.start()

    tp_copy.wait_send()
    weights.wait_send()
    remote(tbuf.at[pl.ds(0, 2 * ZS - 1)], tbuf.at[pl.ds(0, 2 * ZS - 1)], ag_s, ag_r.at[s], partner).wait_send()
    queries_in.wait_send()
    swap.wait_send()
    slots_in.wait_send()
    results = remote(rbuf.at[pl.ds(0, moved)], out.at[:, pl.ds(0, (group - 1) * hd)], r_s, r_r, partner)
    results.wait_send()
    results.wait_recv()
    own.wait()


def shards(ffn_hidden, ffn_weight, residual, norm_gain, kv_weight, destination, queries):
    rows, hidden = ffn_hidden.shape
    feat = ffn_weight.shape[1]
    width = kv_weight.shape[0]
    pair = kv_weight.shape[1] * kv_weight.shape[2]
    clips = destination.shape[0] // rows
    slots = clips * CAPACITY
    tokens = queries.shape[0]
    blocks = width // feat
    group = queries.shape[1] // 128
    half = rows // 2
    dma = pltpu.SemaphoreType.DMA
    return pl.pallas_call(
        kernel,
        out_shape=jax.ShapeDtypeStruct(queries.shape, BF16),
        in_specs=[pl.BlockSpec(memory_space=pl.ANY)] * 7,
        out_specs=pl.BlockSpec(memory_space=pl.ANY),
        scratch_shapes=[
            pltpu.VMEM((rows, hidden), BF16),
            pltpu.VMEM((hidden, feat), BF16),
            pltpu.VMEM((rows, feat), BF16),
            pltpu.VMEM((1, width), F32),
            pltpu.VMEM((2, width, pair), BF16),
            pltpu.VMEM((clips, rows), jnp.int32),
            pltpu.VMEM((slots, rows), BF16),
            pltpu.VMEM((1, slots), F32),
            pltpu.VMEM((rows, feat), F32),
            pltpu.VMEM((half, feat), F32),
            pltpu.VMEM((blocks, half, feat), BF16),
            pltpu.VMEM((blocks, half, feat), BF16),
            pltpu.VMEM((half, pair), BF16),
            pltpu.VMEM((rows, pair), BF16),
            pltpu.VMEM((slots, pair), BF16),
            pltpu.VMEM((slots, pair), BF16),
            pltpu.VMEM((pair // 2, slots), BF16),
            pltpu.VMEM((group * tokens, 128), BF16),
            pltpu.VMEM((group * tokens, 128), BF16),
            dma((8,)),
            dma,
            dma,
            dma,
            dma,
            dma,
            dma((blocks,)),
            dma,
            dma,
            dma,
            dma,
            dma,
            dma,
            dma,
            dma,
        ],
        compiler_params=pltpu.CompilerParams(
            collective_id=0, has_side_effects=True, vmem_limit_bytes=56 * 1024 * 1024
        ),
    )(
        ffn_hidden,
        ffn_weight,
        residual,
        norm_gain.reshape(1, width),
        kv_weight.reshape(width, pair),
        destination.reshape(clips, rows),
        queries,
    )


def solution(mesh):
    return jax.shard_map(
        shards,
        mesh=mesh,
        in_specs=(
            P("clip", "tp"),
            P("tp", "seq"),
            P("clip", "seq"),
            P(),
            P(None, ("seq", "tp"), None),
            P(),
            P(("clip", "seq", "tp"), None),
        ),
        out_specs=P(("clip", "seq", "tp"), None),
        check_vma=False,
    )
```

time: 264 us -> 97.1 us (0.37)
  waiting for transfers between devices: 107 us -> 0 us
  Pallas kernels: 0 us -> 94.6 us
  blocking collectives: 66.4 us -> 0 us
  local copies, waits for them, and re-layouts: 45.9 us -> 2.29 us
  between operations: 13.5 us -> 0.01 us
  matrix products: 11.9 us -> 0 us
  starting transfers between devices: 11.6 us -> 0 us
  other arithmetic: 6.29 us -> 0 us
    pallas_call x0 -> x1, Pallas kernels: none -> 94.6 us  [shards(): pl.pallas_call(kernel, out_shape=jax.ShapeDtypeStruct(queries.shape, BF16...]
    all_to_all x2 -> x0, blocking collectives: 66.4 us -> none  [the longest x1 44.7 us: shards(): lax.all_to_all(result, ('seq', 'tp'), split_axis=1, concat_axis=2, tiled=...]
    psum x1 -> x0, waiting for transfers between devices: 54.2 us -> none  [shards(): summed = lax.psum(partial_value, 'tp')]
    all_to_all x1 -> x0, waiting for transfers between devices: 31.9 us -> none  [shards(): lax.all_to_all(stacked, ('seq', 'tp'), split_axis=2, concat_axis=1, tiled...]
    unnamed x12 -> x1, local copies, waits for them, and re-layouts: 24.6 us -> 2.29 us
    all_gather x1 -> x0, waiting for transfers between devices: 20.7 us -> none  [shards(): full_text = lax.all_gather(arrived, 'seq', axis=1, tiled=True)]
    dot_general x5 -> x0, matrix products: 11.9 us -> none  [the longest x1 4.17 us: shards(): jnp.dot(normed, weight_flat, preferred_element_type=jnp.float32)]
    all_to_all x1 -> x0, starting transfers between devices: 11.6 us -> none  [shards(): lax.all_to_all(stacked, ('seq', 'tp'), split_axis=2, concat_axis=1, tiled...]
  transfers between devices with their start and end apart: 3 -> 0, of which waited for: 3 -> 0; matrix products, arithmetic and copies ran while one was open for 15% -> 0% of each run, Pallas kernels for 0% -> 0%
where the time goes in v1:
time: 97.1 us; the launch traced here: 96.9 us
  Pallas kernels  94.6 us (97%)
  local copies, waits for them, and re-layouts  2.29 us (2%)
    pallas_call x1, Pallas kernels, shards(): pl.pallas_call(kernel, out_shape=jax.ShapeDtypeStruct(queries.shape, BF16...  94.6 us
    unnamed x1, local copies, waits for them, and re-layouts  2.29 us

profile of v1, /device:TPU:1, one launch (start us, length us, event | category | flops | bytes accessed | tf_op | source)
XLA Modules:
  0.0 96.9 jit_solution(729678858973202365)
XLA Ops:
  0.0 94.6 %shard_map.73 = bf16[128,4096]{1,0:T(8,128)(2,1)} custom-call(bf16[128,5120]{1,0:T(8,128)(2,1)} %hid.1, bf16[5120,256]{1,0:T(8,128)(2,1)} %wt.1, bf16[128,256]{1,0:T(8,128)(2,1)} %res.1, f32[1,4096]{1,0:T(1,128)} %bitcast.4, bf16[4096,256]{1,0:T(8,128)(2,1)} %bitcast.3, s32[32,128]{1,0:T(8,128)} %bitcast.5, bf16[128,4096]{1,0:T(8,128)(2,1)} %qry.1), custom_call_target="tpu_custom_call" | custom-call | tf_op jit(solution)/shard_map/pallas_call | solution.py:323
  94.6 2.3 %copy.9 = bf16[128,4096]{1,0:T(8,128)(2,1)} copy(bf16[128,4096]{1,0:T(8,128)(2,1)} %shard_map.73) | data formatting | bytes 2097152

commit v2 on v1

v2 whole, which is shorter than its diff:
```python
import math

import jax
import jax.numpy as jnp
from jax import lax
from jax.experimental import pallas as pl
from jax.experimental.pallas import tpu as pltpu
from jax.sharding import PartitionSpec as P

EPSILON = 1e-06
MESH = pl.DeviceIdType.MESH
F32 = jnp.float32
BF16 = jnp.bfloat16
CAPACITY = 16
ZS = 8
XS = 8


def remote(src, dst, send_sem, recv_sem, device):
    return pltpu.make_async_remote_copy(
        src_ref=src,
        dst_ref=dst,
        send_sem=send_sem,
        recv_sem=recv_sem,
        device_id=device,
        device_id_type=MESH,
    )


def ring_step(k):
    return 4 + (1 - 2 * (k % 2)) * ((k + 1) // 2)


def near_step(k):
    return (1 - 2 * (k % 2)) * ((k + 1) // 2)


def gray(i):
    return i + (i // 2) * (1 - 2 * (i % 2))


def kernel(
    hid,
    wt,
    res,
    gain,
    kvw,
    dest,
    qry,
    out,
    hid_v,
    wt_v,
    res_v,
    gain_v,
    w2_v,
    dest_v,
    sel_v,
    bias_v,
    part,
    part_in,
    tbuf,
    nbuf,
    kv_out,
    kv_rows,
    packed,
    kvall,
    kt_v,
    qbuf,
    rbuf,
    ld,
    tp_s,
    tp_r,
    w_s,
    w_r,
    ag_s,
    ag_r,
    q_s,
    q_r,
    kx_s,
    kx_r,
    c_s,
    c_r,
    k_s,
    k_r,
    r_s,
    r_r,
):
    clips = lax.axis_size("clip")
    c, s, t = lax.axis_index("clip"), lax.axis_index("seq"), lax.axis_index("tp")
    y, z = s // ZS, s % ZS
    yh, x = c // XS, c % XS
    parts = clips // XS
    other = 1 - t
    partner = (c, s, other)
    across = (1 - y) * ZS + z
    member = 2 * y + t
    rows = hid_v.shape[0]
    half = rows // 2
    feat = part.shape[1]
    blocks = tbuf.shape[0]
    hd = 128
    chunk = XS * CAPACITY

    barrier = pltpu.get_barrier_semaphore()

    def greet(device):
        pl.semaphore_signal(barrier, inc=1, device_id=device, device_id_type=MESH)

    @pl.loop(1, ZS)
    def _(o):
        greet((c, y * ZS + (z + o) % ZS, t))

    greet(partner)
    greet((c, across, t))
    greet((c, across, other))

    @pl.loop(1, clips)
    def _(o):
        greet(((c + o) % clips, s, t))

    def column(j):
        return pl.ds(pl.multiple_of(j * hd, hd), hd)

    def block_rows(j, size):
        return pl.ds(pl.multiple_of(j * size, size), size)

    loads = [
        pltpu.make_async_copy(dest, dest_v, ld.at[0]),
        pltpu.make_async_copy(hid, hid_v, ld.at[1]),
        pltpu.make_async_copy(wt, wt_v, ld.at[2]),
        pltpu.make_async_copy(res, res_v, ld.at[3]),
        pltpu.make_async_copy(gain, gain_v, ld.at[4]),
        pltpu.make_async_copy(kvw, w2_v.at[t], ld.at[5]),
    ]
    for load in loads:
        load.start()

    @pl.loop(0, ZS)
    def _(k):
        pltpu.make_async_copy(
            qry.at[:, column(2 * (y * ZS + k) + t)],
            qbuf.at[k, block_rows(member, rows)],
            ld.at[6],
        ).start()

    loads[0].wait()
    dest_row = dest_v[pl.ds(c, 1), :]
    clip_ids = lax.broadcasted_iota(jnp.int32, (clips, rows), 0)
    onehot = jnp.where(clip_ids == dest_row, 1.0, 0.0)
    earlier = jnp.where(
        lax.broadcasted_iota(jnp.int32, (rows, rows), 0)
        < lax.broadcasted_iota(jnp.int32, (rows, rows), 1),
        1.0,
        0.0,
    ).astype(BF16)
    before = jnp.dot(onehot.astype(BF16), earlier, preferred_element_type=F32)
    rank = jnp.sum(before * onehot, axis=0, keepdims=True)
    place = dest_row * CAPACITY + rank.astype(jnp.int32)
    slots = clips * CAPACITY
    target = lax.broadcasted_iota(jnp.int32, (slots, rows), 0)
    sel_v[...] = jnp.where(target == place, 1.0, 0.0).astype(BF16)
    counts = jnp.sum(jnp.where(dest_v[...] == c, 1.0, 0.0), axis=1, keepdims=True)
    slot = lax.broadcasted_iota(jnp.int32, (clips, slots), 1)
    source = lax.broadcasted_iota(jnp.int32, (clips, slots), 0)
    in_block = jnp.where(slot // CAPACITY == source, counts, 0.0)
    filled = jnp.sum(in_block, axis=0, keepdims=True)
    position = (lax.broadcasted_iota(jnp.int32, (1, slots), 1) % CAPACITY).astype(F32)
    bias_v[...] = jnp.where(position < filled, 0.0, -1e30)

    loads[1].wait()
    loads[2].wait()
    step = 1024
    part[...] = jnp.zeros_like(part)

    @pl.loop(0, hid_v.shape[1] // step)
    def _(k):
        at = pl.ds(pl.multiple_of(k * step, step), step)
        part[...] += jnp.dot(hid_v[:, at], wt_v[at, :], preferred_element_type=F32)

    pl.semaphore_wait(barrier, ZS - 1 + 3 + clips - 1)

    tp_copy = remote(part.at[block_rows(other, half)], part_in, tp_s, tp_r, partner)
    tp_copy.start()
    loads[3].wait()
    loads[4].wait()
    tp_copy.wait_recv()
    mine = part[block_rows(t, half), :] + part_in[...]
    text = res_v[block_rows(t, half), :].astype(F32) + mine
    tbuf[s] = text.astype(BF16)

    def text_copy(block, device):
        return remote(tbuf.at[block], tbuf.at[block], ag_s, ag_r.at[block], device)

    @pl.loop(0, ZS - 1)
    def _(k):
        text_copy(s, (c, y * ZS + (z + ring_step(k)) % ZS, t)).start()

    text_copy(s, (c, across, t)).start()

    def send_queries(k):
        at = (z + near_step(k) + ZS) % ZS
        for peer_y, peer_t in ((1 - y, t), (1 - y, other), (y, other)):
            remote(
                qry.at[:, column(2 * (peer_y * ZS + at) + peer_t)],
                qbuf.at[at, block_rows(member, rows)],
                q_s,
                q_r.at[at],
                (c, peer_y * ZS + z, peer_t),
            ).start()

    @pl.loop(0, 2)
    def _(k):
        send_queries(k)

    weights = remote(kvw, w2_v.at[t], w_s, w_r, partner)
    weights.start()

    @pl.loop(0, ZS - 1)
    def _(k):
        block = y * ZS + (z + ring_step(ZS - 2 - k)) % ZS
        text_copy(block, (c, across, t)).wait_recv()
        text_copy(block, (c, across, t)).start()

    @pl.loop(2, ZS)
    def _(k):
        send_queries(k)

    @pl.loop(0, ZS)
    def _(k):
        text_copy((1 - y) * ZS + k, (c, across, t)).wait_recv()

    def squares(b, acc):
        wide = tbuf[b].astype(F32)
        return acc + wide * wide

    total = lax.fori_loop(0, blocks, squares, jnp.zeros((half, feat), F32))
    mean = jnp.sum(total, axis=1, keepdims=True) / (blocks * feat)
    scale = lax.rsqrt(mean + EPSILON)

    @pl.loop(0, blocks)
    def _(b):
        at = pl.ds(pl.multiple_of(b * feat, feat), feat)
        nbuf[:, at] = (tbuf[b].astype(F32) * scale * gain_v[:, at]).astype(BF16)

    def project(head):
        acc = jnp.zeros((half, 2 * hd), F32)
        for k in range(blocks * feat // step):
            at = pl.ds(k * step, step)
            acc += jnp.dot(nbuf[:, at], w2_v[head, at, :], preferred_element_type=F32)
        return acc.astype(BF16)

    weights.wait_recv()
    kv_out[...] = project(other)
    swap = remote(kv_out, kv_rows.at[block_rows(t, half)], kx_s, kx_r, partner)
    swap.start()
    loads[5].wait()
    kv_rows[block_rows(t, half), :] = project(t)
    remote(kv_out, kv_rows.at[block_rows(other, half)], kx_s, kx_r, partner).wait_recv()

    @pl.loop(0, parts)
    def _(i):
        to = (yh + gray(i)) % parts
        at = block_rows(to, chunk)
        packed[at, :] = jnp.dot(sel_v[at, :], kv_rows[...], preferred_element_type=F32).astype(BF16)

        @pl.loop(0, XS)
        def _(j):
            d = to * XS + (x + XS // 2 + j) % XS

            @pl.when(d != c)
            def _():
                remote(
                    packed.at[block_rows(d, CAPACITY)],
                    kvall.at[z, block_rows(c, CAPACITY)],
                    c_s,
                    c_r.at[i],
                    (d, s, t),
                ).start()

    stay = pltpu.make_async_copy(
        packed.at[block_rows(c, CAPACITY)], kvall.at[z, block_rows(c, CAPACITY)], ld.at[7]
    )
    stay.start()
    own_queries = pltpu.make_async_copy(qbuf.at[pl.ds(0, 2)], qbuf.at[pl.ds(0, 2)], ld.at[6])
    own_queries.wait()
    stay.wait()

    factor = 1.0 / math.sqrt(hd)
    up, down = (c, y * ZS + (z + 1) % ZS, t), (c, y * ZS + (z + ZS - 1) % ZS, t)

    def chunk_copy(place, i, device):
        at = block_rows((yh - gray(i) + parts) % parts, chunk)
        piece = kvall.at[place, at]
        return remote(piece, piece, k_s, k_r.at[place * parts + i], device)

    def arrived(i, size):
        piece = kvall.at[z, pl.ds(0, size)]
        remote(packed.at[pl.ds(0, size)], piece, c_s, c_r.at[i], partner).wait_recv()

    def unit_of(n):
        e, i = n // parts - 1, n % parts
        return (z + (2 * (i // 2) - 1) * e + ZS) % ZS, i % 2

    def is_unit(n):
        return (n >= parts) & ((n < parts + 2) | (n >= 2 * parts))

    def result_copy(place, peer_y, peer_t):
        return remote(
            rbuf.at[place, block_rows(2 * peer_y + peer_t, rows)],
            out.at[:, column(2 * (y * ZS + place) + t)],
            r_s,
            r_r,
            (c, peer_y * ZS + z, peer_t),
        )

    def send_unit(n):
        place, peer_y = unit_of(n)

        @pl.when(peer_y == y)
        def _():
            result_copy(place, y, other).start()
            pltpu.make_async_copy(
                rbuf.at[place, block_rows(member, rows)],
                out.at[:, column(2 * (y * ZS + place) + t)],
                ld.at[8],
            ).start()

        @pl.when(peer_y != y)
        def _():
            result_copy(place, 1 - y, t).start()
            result_copy(place, 1 - y, other).start()

    last = parts * (ZS // 2 + 1) + 1

    @pl.loop(0, last + 1)
    def _(n):
        d, i = n // parts, n % parts
        low, high = (z - d + ZS) % ZS, (z + d) % ZS

        @pl.when(n == 0)
        def _():
            arrived(i, chunk - CAPACITY)

        @pl.when((n > 0) & (d == 0))
        def _():
            arrived(i, chunk)

        @pl.when((d > 0) & ((d < ZS // 2) | (n < last - 1)))
        def _():
            chunk_copy(low, i, up).wait_recv()

        @pl.when((d < 3) | ((d == 3) & (i < 2)))
        def _():
            chunk_copy(low, i, up).start()

        @pl.when((d > 0) & (d < ZS // 2))
        def _():
            chunk_copy(high, i, down).wait_recv()

        @pl.when((d < 3) | ((d == 3) & (i >= 2)))
        def _():
            chunk_copy(high, i, down).start()

        @pl.when(is_unit(n - 1))
        def _():
            send_unit(n - 1)

        @pl.when(is_unit(n))
        def _():
            place, peer_y = unit_of(n)

            @pl.when(i % 2 == 0)
            def _():
                into = qbuf.at[place, pl.ds(0, 3 * rows)]
                remote(into, into, q_s, q_r.at[place], partner).wait_recv()
                kt_v[...] = kvall[place, :, :hd].T

            tokens = block_rows(peer_y, 2 * rows)
            scores = jnp.dot(qbuf[place, tokens, :], kt_v[...], preferred_element_type=F32)
            scores = scores * factor + bias_v[...]
            peak = jnp.max(scores, axis=1, keepdims=True)
            w = jnp.exp(scores - peak)
            probs = (w * (1.0 / jnp.sum(w, axis=1, keepdims=True))).astype(BF16)
            attended = jnp.dot(probs, kvall[place, :, hd:], preferred_element_type=F32)
            rbuf[place, tokens, :] = attended.astype(BF16)

    tp_copy.wait_send()
    weights.wait_send()
    remote(tbuf.at[pl.ds(0, 2 * ZS - 1)], tbuf.at[pl.ds(0, 2 * ZS - 1)], ag_s, ag_r.at[s], partner).wait_send()
    swap.wait_send()
    remote(packed.at[pl.ds(0, slots - CAPACITY)], packed.at[pl.ds(0, slots - CAPACITY)], c_s, c_r.at[0], partner).wait_send()
    send_unit(last)
    most = pl.ds(0, 3 * ZS // 4)
    remote(qbuf.at[most], qbuf.at[most], q_s, q_r.at[0], partner).wait_send()
    remote(kvall.at[pl.ds(0, ZS - 1)], kvall.at[pl.ds(0, ZS - 1)], k_s, k_r.at[0], partner).wait_send()
    here = out.at[:, pl.ds(0, ZS * hd)]
    pltpu.make_async_copy(here, here, ld.at[8]).wait()
    results = remote(rbuf.at[most], out.at[:, pl.ds(0, 3 * ZS * hd)], r_s, r_r, partner)
    results.wait_send()
    results.wait_recv()


def shards(ffn_hidden, ffn_weight, residual, norm_gain, kv_weight, destination, queries):
    rows, hidden = ffn_hidden.shape
    feat = ffn_weight.shape[1]
    width = kv_weight.shape[0]
    pair = kv_weight.shape[1] * kv_weight.shape[2]
    clips = destination.shape[0] // rows
    slots = clips * CAPACITY
    tokens = queries.shape[0]
    blocks = width // feat
    half = rows // 2
    dma = pltpu.SemaphoreType.DMA
    return pl.pallas_call(
        kernel,
        out_shape=jax.ShapeDtypeStruct(queries.shape, BF16),
        in_specs=[pl.BlockSpec(memory_space=pl.ANY)] * 7,
        out_specs=pl.BlockSpec(memory_space=pl.ANY),
        scratch_shapes=[
            pltpu.VMEM((rows, hidden), BF16),
            pltpu.VMEM((hidden, feat), BF16),
            pltpu.VMEM((rows, feat), BF16),
            pltpu.VMEM((1, width), F32),
            pltpu.VMEM((2, width, pair), BF16),
            pltpu.VMEM((clips, rows), jnp.int32),
            pltpu.VMEM((slots, rows), BF16),
            pltpu.VMEM((1, slots), F32),
            pltpu.VMEM((rows, feat), F32),
            pltpu.VMEM((half, feat), F32),
            pltpu.VMEM((blocks, half, feat), BF16),
            pltpu.VMEM((half, width), BF16),
            pltpu.VMEM((half, pair), BF16),
            pltpu.VMEM((rows, pair), BF16),
            pltpu.VMEM((slots, pair), BF16),
            pltpu.VMEM((ZS, slots, pair), BF16),
            pltpu.VMEM((pair // 2, slots), BF16),
            pltpu.VMEM((ZS, 4 * tokens, 128), BF16),
            pltpu.VMEM((ZS, 4 * tokens, 128), BF16),
            dma((9,)),
            dma,
            dma,
            dma,
            dma,
            dma,
            dma((blocks,)),
            dma,
            dma((ZS,)),
            dma,
            dma,
            dma,
            dma((clips // XS,)),
            dma,
            dma((ZS * clips // XS,)),
            dma,
            dma,
        ],
        compiler_params=pltpu.CompilerParams(
            collective_id=0, has_side_effects=True, vmem_limit_bytes=56 * 1024 * 1024
        ),
    )(
        ffn_hidden,
        ffn_weight,
        residual,
        norm_gain.reshape(1, width),
        kv_weight.reshape(width, pair),
        destination.reshape(clips, rows),
        queries,
    )


def solution(mesh):
    return jax.shard_map(
        shards,
        mesh=mesh,
        in_specs=(
            P("clip", "tp"),
            P("tp", "seq"),
            P("clip", "seq"),
            P(),
            P(None, ("seq", "tp"), None),
            P(),
            P(("clip", "seq", "tp"), None),
        ),
        out_specs=P(("clip", "seq", "tp"), None),
        check_vma=False,
    )
```

time: 97.1 us -> 83.1 us (0.86)
  Pallas kernels: 94.6 us -> 80.4 us
    pallas_call x1, Pallas kernels: 94.6 us -> 80.4 us  [shards(): pl.pallas_call(kernel, out_shape=jax.ShapeDtypeStruct(queries.shape, BF16...]
where the time goes in v2:
time: 83.1 us; the launch traced here: 82.7 us
  Pallas kernels  80.4 us (97%)
  local copies, waits for them, and re-layouts  2.29 us (3%)
    pallas_call x1, Pallas kernels, shards(): pl.pallas_call(kernel, out_shape=jax.ShapeDtypeStruct(queries.shape, BF16...  80.4 us
    unnamed x1, local copies, waits for them, and re-layouts  2.29 us

profile of v2, /device:TPU:1, one launch (start us, length us, event | category | flops | bytes accessed | tf_op | source)
XLA Modules:
  0.0 82.7 jit_solution(14999902179555075869)
XLA Ops:
  0.0 80.4 %shard_map.73 = bf16[128,4096]{1,0:T(8,128)(2,1)} custom-call(bf16[128,5120]{1,0:T(8,128)(2,1)} %hid.1, bf16[5120,256]{1,0:T(8,128)(2,1)} %wt.1, bf16[128,256]{1,0:T(8,128)(2,1)} %res.1, f32[1,4096]{1,0:T(1,128)} %bitcast.4, bf16[4096,256]{1,0:T(8,128)(2,1)} %bitcast.3, s32[32,128]{1,0:T(8,128)} %bitcast.5, bf16[128,4096]{1,0:T(8,128)(2,1)} %qry.1), custom_call_target="tpu_custom_call" | custom-call | tf_op jit(solution)/shard_map/pallas_call | solution.py:414
  80.4 2.3 %copy.9 = bf16[128,4096]{1,0:T(8,128)(2,1)} copy(bf16[128,4096]{1,0:T(8,128)(2,1)} %shard_map.73) | data formatting | bytes 2097152

commit v3 on v2

--- a/solution.py
+++ b/solution.py
@@ -12,6 +12,7 @@
 F32 = jnp.float32
 BF16 = jnp.bfloat16
 CAPACITY = 16
+EARLY = 1
 ZS = 8
 XS = 8
 
@@ -25,10 +26,6 @@
         device_id=device,
         device_id_type=MESH,
     )
-
-
-def ring_step(k):
-    return 4 + (1 - 2 * (k % 2)) * ((k + 1) // 2)
 
 
 def near_step(k):
@@ -106,17 +103,21 @@
     def greet(device):
         pl.semaphore_signal(barrier, inc=1, device_id=device, device_id_type=MESH)
 
+    @pl.loop(0, clips)
+    def _(o):
+        to = (yh + 2 + o // XS) % parts * XS + (x + XS // 2 + o) % XS
+
+        @pl.when(to != c)
+        def _():
+            greet((to, s, t))
+
     @pl.loop(1, ZS)
     def _(o):
         greet((c, y * ZS + (z + o) % ZS, t))
 
-    greet(partner)
     greet((c, across, t))
     greet((c, across, other))
-
-    @pl.loop(1, clips)
-    def _(o):
-        greet(((c + o) % clips, s, t))
+    greet(partner)
 
     def column(j):
         return pl.ds(pl.multiple_of(j * hd, hd), hd)
@@ -124,15 +125,17 @@
     def block_rows(j, size):
         return pl.ds(pl.multiple_of(j * size, size), size)
 
-    loads = [
-        pltpu.make_async_copy(dest, dest_v, ld.at[0]),
-        pltpu.make_async_copy(hid, hid_v, ld.at[1]),
-        pltpu.make_async_copy(wt, wt_v, ld.at[2]),
-        pltpu.make_async_copy(res, res_v, ld.at[3]),
-        pltpu.make_async_copy(gain, gain_v, ld.at[4]),
-        pltpu.make_async_copy(kvw, w2_v.at[t], ld.at[5]),
-    ]
-    for load in loads:
+    step = 1024
+    depths = [pl.ds(k * step, step) for k in range(hid_v.shape[1] // step)]
+    loads = []
+    for k, at in enumerate(depths):
+        loads.append(pltpu.make_async_copy(hid.at[:, at], hid_v.at[:, at], ld.at[9 + 2 * k]))
+        loads.append(pltpu.make_async_copy(wt.at[at], wt_v.at[at], ld.at[10 + 2 * k]))
+    dest_load = pltpu.make_async_copy(dest, dest_v, ld.at[0])
+    res_load = pltpu.make_async_copy(res, res_v, ld.at[3])
+    gain_load = pltpu.make_async_copy(gain, gain_v, ld.at[4])
+    w_load = pltpu.make_async_copy(kvw, w2_v.at[t], ld.at[5])
+    for load in loads + [res_load, dest_load, gain_load, w_load]:
         load.start()
 
     @pl.loop(0, ZS)
@@ -143,7 +146,50 @@
             ld.at[6],
         ).start()
 
-    loads[0].wait()
+    total = jnp.zeros(part.shape, F32)
+    for k, at in enumerate(depths):
+        loads[2 * k].wait()
+        loads[2 * k + 1].wait()
+        total += jnp.dot(hid_v[:, at], wt_v[at, :], preferred_element_type=F32)
+    part[...] = total
+
+    pl.semaphore_wait(barrier, ZS - 1 + 3 + clips - 1)
+
+    tp_copy = remote(part.at[block_rows(other, half)], part_in, tp_s, tp_r, partner)
+    tp_copy.start()
+    res_load.wait()
+    tp_copy.wait_recv()
+    mine = part[block_rows(t, half), :] + part_in[...]
+    text = res_v[block_rows(t, half), :].astype(F32) + mine
+    tbuf[s] = text.astype(BF16)
+
+    def text_copy(block, device):
+        return remote(tbuf.at[block], tbuf.at[block], ag_s, ag_r.at[block], device)
+
+    def along(d):
+        return y * ZS + (z + d + ZS) % ZS
+
+    def pass_on(block, to):
+        text_copy(block, (c, to, t)).start()
+
+    for to in (across, along(-1), along(1), along(-2), along(2)):
+        pass_on(s, to)
+
+    def send_queries(k):
+        at = (z + near_step(k) + ZS) % ZS
+        for peer_y, peer_t in ((1 - y, t), (1 - y, other), (y, other)):
+            remote(
+                qry.at[:, column(2 * (peer_y * ZS + at) + peer_t)],
+                qbuf.at[at, block_rows(member, rows)],
+                q_s,
+                q_r.at[at],
+                (c, peer_y * ZS + z, peer_t),
+            ).start()
+
+    weights = remote(kvw, w2_v.at[t], w_s, w_r, partner)
+    weights.start()
+
+    dest_load.wait()
     dest_row = dest_v[pl.ds(c, 1), :]
     clip_ids = lax.broadcasted_iota(jnp.int32, (clips, rows), 0)
     onehot = jnp.where(clip_ids == dest_row, 1.0, 0.0)
@@ -167,67 +213,28 @@
     position = (lax.broadcasted_iota(jnp.int32, (1, slots), 1) % CAPACITY).astype(F32)
     bias_v[...] = jnp.where(position < filled, 0.0, -1e30)
 
-    loads[1].wait()
-    loads[2].wait()
-    step = 1024
-    part[...] = jnp.zeros_like(part)
-
-    @pl.loop(0, hid_v.shape[1] // step)
-    def _(k):
-        at = pl.ds(pl.multiple_of(k * step, step), step)
-        part[...] += jnp.dot(hid_v[:, at], wt_v[at, :], preferred_element_type=F32)
-
-    pl.semaphore_wait(barrier, ZS - 1 + 3 + clips - 1)
-
-    tp_copy = remote(part.at[block_rows(other, half)], part_in, tp_s, tp_r, partner)
-    tp_copy.start()
-    loads[3].wait()
-    loads[4].wait()
-    tp_copy.wait_recv()
-    mine = part[block_rows(t, half), :] + part_in[...]
-    text = res_v[block_rows(t, half), :].astype(F32) + mine
-    tbuf[s] = text.astype(BF16)
-
-    def text_copy(block, device):
-        return remote(tbuf.at[block], tbuf.at[block], ag_s, ag_r.at[block], device)
-
-    @pl.loop(0, ZS - 1)
-    def _(k):
-        text_copy(s, (c, y * ZS + (z + ring_step(k)) % ZS, t)).start()
-
-    text_copy(s, (c, across, t)).start()
-
-    def send_queries(k):
-        at = (z + near_step(k) + ZS) % ZS
-        for peer_y, peer_t in ((1 - y, t), (1 - y, other), (y, other)):
-            remote(
-                qry.at[:, column(2 * (peer_y * ZS + at) + peer_t)],
-                qbuf.at[at, block_rows(member, rows)],
-                q_s,
-                q_r.at[at],
-                (c, peer_y * ZS + z, peer_t),
-            ).start()
-
-    @pl.loop(0, 2)
-    def _(k):
-        send_queries(k)
-
-    weights = remote(kvw, w2_v.at[t], w_s, w_r, partner)
-    weights.start()
-
-    @pl.loop(0, ZS - 1)
-    def _(k):
-        block = y * ZS + (z + ring_step(ZS - 2 - k)) % ZS
+    for d in (-1, 1, -2, 2, -3, 3, 4):
+        block = along(d)
         text_copy(block, (c, across, t)).wait_recv()
-        text_copy(block, (c, across, t)).start()
-
-    @pl.loop(2, ZS)
-    def _(k):
-        send_queries(k)
+        if d in (-2, 2):
+            onward = -d // 2
+            pass_on(block, along(onward))
+
+            @pl.when(t == (0 if d < 0 else 1))
+            def _(block=block, onward=onward):
+                pass_on(block, along(2 * onward))
+
+        pass_on(block, across)
 
     @pl.loop(0, ZS)
     def _(k):
         text_copy((1 - y) * ZS + k, (c, across, t)).wait_recv()
+
+    @pl.loop(0, EARLY)
+    def _(k):
+        send_queries(k)
+
+    gain_load.wait()
 
     def squares(b, acc):
         wide = tbuf[b].astype(F32)
@@ -253,7 +260,7 @@
     kv_out[...] = project(other)
     swap = remote(kv_out, kv_rows.at[block_rows(t, half)], kx_s, kx_r, partner)
     swap.start()
-    loads[5].wait()
+    w_load.wait()
     kv_rows[block_rows(t, half), :] = project(t)
     remote(kv_out, kv_rows.at[block_rows(other, half)], kx_s, kx_r, partner).wait_recv()
 
@@ -299,7 +306,7 @@
 
     def unit_of(n):
         e, i = n // parts - 1, n % parts
-        return (z + (2 * (i // 2) - 1) * e + ZS) % ZS, i % 2
+        return (z + (2 * (i // 2) - 1) * e + ZS) % ZS, (i + 1 + y) % 2
 
     def is_unit(n):
         return (n >= parts) & ((n < parts + 2) | (n >= 2 * parts))
@@ -360,6 +367,10 @@
         @pl.when((d < 3) | ((d == 3) & (i >= 2)))
         def _():
             chunk_copy(high, i, down).start()
+
+        @pl.when((n >= parts - 1) & (n < parts - 1 + ZS - EARLY))
+        def _():
+            send_queries(n - parts + 1 + EARLY)
 
         @pl.when(is_unit(n - 1))
         def _():
@@ -413,9 +424,9 @@
     dma = pltpu.SemaphoreType.DMA
     return pl.pallas_call(
         kernel,
-        out_shape=jax.ShapeDtypeStruct(queries.shape, BF16),
+        out_shape=pltpu.VMEM(queries.shape, BF16),
         in_specs=[pl.BlockSpec(memory_space=pl.ANY)] * 7,
-        out_specs=pl.BlockSpec(memory_space=pl.ANY),
+        out_specs=pl.BlockSpec(memory_space=pltpu.VMEM),
         scratch_shapes=[
             pltpu.VMEM((rows, hidden), BF16),
             pltpu.VMEM((hidden, feat), BF16),
@@ -436,7 +447,7 @@
             pltpu.VMEM((pair // 2, slots), BF16),
             pltpu.VMEM((ZS, 4 * tokens, 128), BF16),
             pltpu.VMEM((ZS, 4 * tokens, 128), BF16),
-            dma((9,)),
+            dma((9 + 2 * (hidden // 1024),)),
             dma,
             dma,
             dma,

time: 83.1 us -> 76.7 us (0.923)
  Pallas kernels: 80.4 us -> 75.6 us
  local copies, waits for them, and re-layouts: 2.29 us -> 0.97 us
    pallas_call x1, Pallas kernels: 80.4 us -> 75.6 us  [shards(): pl.pallas_call(kernel, out_shape=pltpu.VMEM(queries.shape, BF16), in_spec...]
    unnamed x1, local copies, waits for them, and re-layouts: 2.29 us -> 0.97 us
where the time goes in v3:
time: 76.7 us; the launch traced here: 76.6 us
  Pallas kernels  75.6 us (99%)
  local copies, waits for them, and re-layouts  0.97 us (1%)
    pallas_call x1, Pallas kernels, shards(): pl.pallas_call(kernel, out_shape=pltpu.VMEM(queries.shape, BF16), in_spec...  75.6 us

profile of v3, /device:TPU:1, one launch (start us, length us, event | category | flops | bytes accessed | tf_op | source)
XLA Modules:
  0.0 76.6 jit_solution(2876802273252719499)
XLA Ops:
  0.0 75.6 %shard_map.73 = bf16[128,4096]{1,0:T(8,128)(2,1)S(1)} custom-call(bf16[128,5120]{1,0:T(8,128)(2,1)} %hid.1, bf16[5120,256]{1,0:T(8,128)(2,1)} %wt.1, bf16[128,256]{1,0:T(8,128)(2,1)} %res.1, f32[1,4096]{1,0:T(1,128)} %bitcast.4, bf16[4096,256]{1,0:T(8,128)(2,1)} %bitcast.3, s32[32,128]{1,0:T(8,128)} %bitcast.5, bf16[128,4096]{1,0:T(8,128)(2,1)} %qry.1), custom_call_target="tpu_custom_call" | custom-call | tf_op jit(solution)/shard_map/pallas_call | solution.py:425
  75.6 1.0 %copy.9 = bf16[128,4096]{1,0:T(8,128)(2,1)} copy(bf16[128,4096]{1,0:T(8,128)(2,1)S(1)} %shard_map.73) | data formatting | bytes 2097152

commit v4 on v3

--- a/solution.py
+++ b/solution.py
@@ -12,7 +12,8 @@
 F32 = jnp.float32
 BF16 = jnp.bfloat16
 CAPACITY = 16
-EARLY = 1
+AT_START, IN_GATHER = 1, 2
+EARLY = 4
 ZS = 8
 XS = 8
 
@@ -81,6 +82,7 @@
     k_r,
     r_s,
     r_r,
+    ready,
 ):
     clips = lax.axis_size("clip")
     c, s, t = lax.axis_index("clip"), lax.axis_index("seq"), lax.axis_index("tp")
@@ -98,27 +100,6 @@
     hd = 128
     chunk = XS * CAPACITY
 
-    barrier = pltpu.get_barrier_semaphore()
-
-    def greet(device):
-        pl.semaphore_signal(barrier, inc=1, device_id=device, device_id_type=MESH)
-
-    @pl.loop(0, clips)
-    def _(o):
-        to = (yh + 2 + o // XS) % parts * XS + (x + XS // 2 + o) % XS
-
-        @pl.when(to != c)
-        def _():
-            greet((to, s, t))
-
-    @pl.loop(1, ZS)
-    def _(o):
-        greet((c, y * ZS + (z + o) % ZS, t))
-
-    greet((c, across, t))
-    greet((c, across, other))
-    greet(partner)
-
     def column(j):
         return pl.ds(pl.multiple_of(j * hd, hd), hd)
 
@@ -135,7 +116,33 @@
     res_load = pltpu.make_async_copy(res, res_v, ld.at[3])
     gain_load = pltpu.make_async_copy(gain, gain_v, ld.at[4])
     w_load = pltpu.make_async_copy(kvw, w2_v.at[t], ld.at[5])
-    for load in loads + [res_load, dest_load, gain_load, w_load]:
+    for load in loads:
+        load.start()
+
+    barrier = pltpu.get_barrier_semaphore()
+
+    def greet(device):
+        pl.semaphore_signal(barrier, inc=1, device_id=device, device_id_type=MESH)
+
+    @pl.loop(1, parts)
+    def _(o):
+        greet(((yh + o) % parts * XS + x, s, t))
+
+    @pl.loop(1, XS)
+    def _(o):
+        greet((yh * XS + (x + o) % XS, s, t))
+
+    @pl.loop(1, ZS)
+    def _(o):
+        greet((c, y * ZS + (z + o) % ZS, t))
+
+    for d in (-2, -1, 0, 1, 2):
+        greet((c, (1 - y) * ZS + (z + d + ZS) % ZS, t))
+
+    greet((c, across, other))
+    greet(partner)
+
+    for load in (res_load, dest_load, gain_load, w_load):
         load.start()
 
     @pl.loop(0, ZS)
@@ -153,7 +160,12 @@
         total += jnp.dot(hid_v[:, at], wt_v[at, :], preferred_element_type=F32)
     part[...] = total
 
-    pl.semaphore_wait(barrier, ZS - 1 + 3 + clips - 1)
+    pl.semaphore_wait(barrier, ZS - 1 + 7 + parts - 1 + XS - 1)
+
+    @pl.loop(1, parts)
+    def _(o):
+        peer = ((yh + o) % parts * XS + x, s, t)
+        pl.semaphore_signal(ready, inc=1, device_id=peer, device_id_type=MESH)
 
     tp_copy = remote(part.at[block_rows(other, half)], part_in, tp_s, tp_r, partner)
     tp_copy.start()
@@ -168,6 +180,9 @@
 
     def along(d):
         return y * ZS + (z + d + ZS) % ZS
+
+    def beside(d):
+        return (1 - y) * ZS + (z + d + ZS) % ZS
 
     def pass_on(block, to):
         text_copy(block, (c, to, t)).start()
@@ -185,6 +200,10 @@
                 q_r.at[at],
                 (c, peer_y * ZS + z, peer_t),
             ).start()
+
+    @pl.loop(0, AT_START)
+    def _(k):
+        send_queries(k)
 
     weights = remote(kvw, w2_v.at[t], w_s, w_r, partner)
     weights.start()
@@ -219,18 +238,26 @@
         if d in (-2, 2):
             onward = -d // 2
             pass_on(block, along(onward))
+            pass_on(block, beside(onward))
 
             @pl.when(t == (0 if d < 0 else 1))
             def _(block=block, onward=onward):
                 pass_on(block, along(2 * onward))
-
-        pass_on(block, across)
+                pass_on(block, beside(2 * onward))
+
+        if abs(d) < 3:
+            pass_on(block, across)
+        if d == 2:
+
+            @pl.loop(AT_START, IN_GATHER)
+            def _(k):
+                send_queries(k)
 
     @pl.loop(0, ZS)
     def _(k):
         text_copy((1 - y) * ZS + k, (c, across, t)).wait_recv()
 
-    @pl.loop(0, EARLY)
+    @pl.loop(IN_GATHER, EARLY)
     def _(k):
         send_queries(k)
 
@@ -263,6 +290,8 @@
     w_load.wait()
     kv_rows[block_rows(t, half), :] = project(t)
     remote(kv_out, kv_rows.at[block_rows(other, half)], kx_s, kx_r, partner).wait_recv()
+
+    pl.semaphore_wait(ready, parts - 1)
 
     @pl.loop(0, parts)
     def _(i):
@@ -308,9 +337,6 @@
         e, i = n // parts - 1, n % parts
         return (z + (2 * (i // 2) - 1) * e + ZS) % ZS, (i + 1 + y) % 2
 
-    def is_unit(n):
-        return (n >= parts) & ((n < parts + 2) | (n >= 2 * parts))
-
     def result_copy(place, peer_y, peer_t):
         return remote(
             rbuf.at[place, block_rows(2 * peer_y + peer_t, rows)],
@@ -337,11 +363,18 @@
             result_copy(place, 1 - y, t).start()
             result_copy(place, 1 - y, other).start()
 
-    last = parts * (ZS // 2 + 1) + 1
+    def order_of(n):
+        m, late = n % 8, (n // 8 + 1) // 2
+        some, end = (m + 7) // 8, m // 7
+        d = some * ((1 - m % 2) * (1 - end) + end)
+        i = some * ((m % 2) * ((m + 1) // 2) + (1 - m % 2) * (m // 2 - 1)) - end
+        return late * (n // parts) + (1 - late) * d, late * (n % parts) + (1 - late) * i
+
+    first, last = 2 * parts - 2, parts * (ZS // 2 + 1) + 1
 
     @pl.loop(0, last + 1)
     def _(n):
-        d, i = n // parts, n % parts
+        d, i = order_of(n)
         low, high = (z - d + ZS) % ZS, (z + d) % ZS
 
         @pl.when(n == 0)
@@ -352,7 +385,7 @@
         def _():
             arrived(i, chunk)
 
-        @pl.when((d > 0) & ((d < ZS // 2) | (n < last - 1)))
+        @pl.when((d > 0) & (d < ZS // 2))
         def _():
             chunk_copy(low, i, up).wait_recv()
 
@@ -368,15 +401,21 @@
         def _():
             chunk_copy(high, i, down).start()
 
-        @pl.when((n >= parts - 1) & (n < parts - 1 + ZS - EARLY))
-        def _():
-            send_queries(n - parts + 1 + EARLY)
-
-        @pl.when(is_unit(n - 1))
+        @pl.when((n >= 5) & (n < 5 + ZS - EARLY))
+        def _():
+            send_queries(n - 5 + EARLY)
+
+        @pl.when(n > first)
         def _():
             send_unit(n - 1)
 
-        @pl.when(is_unit(n))
+        @pl.when(n == last - 1)
+        def _():
+            @pl.loop(0, parts)
+            def _(k):
+                chunk_copy((z + ZS // 2) % ZS, k, up).wait_recv()
+
+        @pl.when(n >= first)
         def _():
             place, peer_y = unit_of(n)
 
@@ -464,6 +503,7 @@
             dma((ZS * clips // XS,)),
             dma,
             dma,
+            pltpu.SemaphoreType.REGULAR,
         ],
         compiler_params=pltpu.CompilerParams(
             collective_id=0, has_side_effects=True, vmem_limit_bytes=56 * 1024 * 1024

time: 76.7 us -> 74.7 us (0.974)
  Pallas kernels: 75.6 us -> 73.6 us
    pallas_call x1, Pallas kernels: 75.6 us -> 73.6 us  [shards(): pl.pallas_call(kernel, out_shape=pltpu.VMEM(queries.shape, BF16), in_spec...]
where the time goes in v4:
time: 74.7 us; the launch traced here: 74.6 us
  Pallas kernels  73.6 us (99%)
  local copies, waits for them, and re-layouts  0.97 us (1%)
    pallas_call x1, Pallas kernels, shards(): pl.pallas_call(kernel, out_shape=pltpu.VMEM(queries.shape, BF16), in_spec...  73.6 us

profile of v4, /device:TPU:1, one launch (start us, length us, event | category | flops | bytes accessed | tf_op | source)
XLA Modules:
  0.0 74.6 jit_solution(17406821431048110527)
XLA Ops:
  0.0 73.6 %shard_map.73 = bf16[128,4096]{1,0:T(8,128)(2,1)S(1)} custom-call(bf16[128,5120]{1,0:T(8,128)(2,1)} %hid.1, bf16[5120,256]{1,0:T(8,128)(2,1)} %wt.1, bf16[128,256]{1,0:T(8,128)(2,1)} %res.1, f32[1,4096]{1,0:T(1,128)} %bitcast.4, bf16[4096,256]{1,0:T(8,128)(2,1)} %bitcast.3, s32[32,128]{1,0:T(8,128)} %bitcast.5, bf16[128,4096]{1,0:T(8,128)(2,1)} %qry.1), custom_call_target="tpu_custom_call" | custom-call | tf_op jit(solution)/shard_map/pallas_call | solution.py:464
  73.6 1.0 %copy.9 = bf16[128,4096]{1,0:T(8,128)(2,1)} copy(bf16[128,4096]{1,0:T(8,128)(2,1)S(1)} %shard_map.73) | data formatting | bytes 2097152
